TPU v7x, 32 devices: a whole 2x2x4 slice. The times are simulated.
32 devices in a mesh: section: 2 (over core), expert: 8 (over z, x), head: 2 (over y).
Axes of the slice: x: 2, y: 2, z: 4, core: 2. Of those that a mesh axis runs over, the one named last changes fastest.
Arguments:
- boundary: bfloat16 [2, 2, 1024, 768], P('section', None, 'expert', 'head'), may hold values from -6 to 6
- norm_gain: float32 [2, 768], P('section'), may hold values from 0.25 to 1.75
- gate_prob: float32 [2, 2, 1024], P('section', None, 'expert'), may hold values from 0.25 to 1
- expert_ids: int32 [2, 2, 1024], P('section', None, 'expert'), may hold values from 0 to 7, as said below
- slot_ids: int32 [2, 2, 1024], P('section', None, 'expert'), may hold values from 0 to 32, as said below
- weight_in: bfloat16 [2, 8, 768, 3072], P('section', 'expert', None, 'head'), may hold values from -0.21875 to 0.21875
- weight_out: bfloat16 [2, 8, 3072, 768], P('section', 'expert', 'head'), may hold values from -0.109375 to 0.109375
Outputs:
- boundary_out: bfloat16 [2, 2, 1024, 768], P('section', None, 'expert', 'head')
- grad_in: bfloat16 [2, 8, 768, 3072], P('section', 'expert', None, 'head')
- grad_out: bfloat16 [2, 8, 3072, 768], P('section', 'expert', 'head')
Inputs may be any that keep to these rules, and one draw needn't show every extreme that they name: `expert_ids`: within each layer and micro-batch, tokens are taken in blocks of 128 (the tokens of one index of expert); in every block one expert, the same for all blocks of that layer and micro-batch, is named by more than 32 tokens. `slot_ids`: A token's slot is the number of earlier tokens of its block that name the same expert, capped at 32; 32 means the token is dropped. So at most 32 tokens of a block hold a slot below 32 at one expert, and in every layer and micro-batch one expert has all 32 slots filled from every block.
All inputs are finite; a program needn't handle non-finite values.
Results may differ from a plain program's by a relative error of at most 0.008.
Values may be sent and summed in bfloat16 or wider, within the bound.
A program may use at most 128 MiB of HBM per device.

v0:
```python
import functools

import jax
import jax.numpy as jnp
from jax import lax
from jax.experimental import pallas as pl
from jax.experimental.pallas import tpu as pltpu
from jax.sharding import PartitionSpec as P

EPSILON = 1e-06
ROOT_COEF = 0.7978845608
CUBE_COEF = 0.044715
MESH = pl.DeviceIdType.MESH
BF16 = jnp.bfloat16
F32 = jnp.float32
FWD, BWD = 0, 1
SQUARE, CROSS = 0, 1
COLS = 256


def activate(pre_act):
    tangent = jnp.tanh(ROOT_COEF * (pre_act + CUBE_COEF * pre_act * pre_act * pre_act))
    act_value = 0.5 * pre_act * (1.0 + tangent)
    act_slope = 0.5 * (1.0 + tangent) + 0.5 * pre_act * (1.0 - tangent * tangent) * ROOT_COEF * (
        1.0 + 3.0 * CUBE_COEF * pre_act * pre_act
    )
    return (act_value, act_slope)


def dot(left, right, dims=((1,), (0,))):
    return lax.dot_general(left, right, (dims, ((), ())), preferred_element_type=F32)


NT = ((1,), (1,))
TN = ((0,), (0,))


def kernel(
    experts, cap, pad,
    local_ref, gain_ref, prob_ref, ids_ref, slots_ref, win_ref, wout_ref,
    out_ref, gin_ref, gout_ref,
    tab, send, rows, normed, act, gpre, mid, keep, away, recvp, back, sec_src, sec_in, xsend, xrecv,
    s1, r1, s2, r2, s3, r3, s4, r4, s5, r5, s6, r6,
):
    sec, me, head = lax.axis_index("section"), lax.axis_index("expert"), lax.axis_index("head")
    other = 1 - head
    micro, tok, half = local_ref.shape
    full = 2 * half
    total = experts * pad
    hidden_half = win_ref.shape[1]
    chunks = hidden_half // COLS
    own_cols = pl.ds(pl.multiple_of(head * half, 128), half)
    other_cols = pl.ds(pl.multiple_of(other * half, 128), half)

    barrier = pltpu.get_barrier_semaphore()

    def each_peer(action):
        def step(k, carry):
            action(lax.rem(me + k, experts))
            return carry

        lax.fori_loop(1, experts, step, 0)

    each_peer(
        lambda d: pl.semaphore_signal(barrier, inc=1, device_id={"expert": d}, device_id_type=MESH)
    )
    pl.semaphore_signal(barrier, inc=1, device_id={"head": other}, device_id_type=MESH)
    pl.semaphore_signal(barrier, inc=1, device_id={"section": 1 - sec}, device_id_type=MESH)

    def slot_rows(index):
        return pl.ds(pl.multiple_of(index * pad, pad), pad)

    def micro_rows(m, index):
        return pl.ds(pl.multiple_of(m * total + index * pad, pad), pad)

    def span(m):
        return slice(m * total, (m + 1) * total)

    eye = lax.broadcasted_iota(jnp.int32, (tok, tok), 0) == lax.broadcasted_iota(
        jnp.int32, (tok, tok), 1
    )

    def to_col(row):
        return jnp.sum(jnp.where(eye, row, 0.0), axis=1, keepdims=True)

    def to_row(col):
        return jnp.sum(jnp.where(eye, col, 0.0), axis=0, keepdims=True)

    for m in range(micro):
        ids, slots = ids_ref[m : m + 1, :], slots_ref[m : m + 1, :]
        target = jnp.where(slots < cap, ids * pad + slots, -1)
        hit = target == lax.broadcasted_iota(jnp.int32, (total, tok), 0)
        tab[m] = jnp.where(hit, 1.0, 0.0).astype(BF16)
    prob = [to_col(prob_ref[m : m + 1, :]) for m in range(micro)]
    gain = gain_ref[...]
    gain_half = gain_ref[:, own_cols]

    def chunk_copy(kind, m, dst, came_from):
        return pltpu.make_async_remote_copy(
            src_ref=send.at[kind, m, slot_rows(dst), :],
            dst_ref=rows.at[kind, micro_rows(m, came_from), own_cols],
            send_sem=s1.at[kind, m, dst],
            recv_sem=r1.at[kind, m, came_from],
            device_id={"expert": dst},
            device_id_type=MESH,
        )

    def relay_copy(kind, m, block, cols):
        return pltpu.make_async_remote_copy(
            src_ref=rows.at[kind, micro_rows(m, block), own_cols],
            dst_ref=rows.at[kind, micro_rows(m, block), cols],
            send_sem=s2.at[kind, m, block],
            recv_sem=r2.at[kind, m, block],
            device_id={"head": other},
            device_id_type=MESH,
        )

    def place(kind, m, tokens):
        send[kind, m] = dot(tab[m], tokens).astype(BF16)

    def dispatch(kind, m):
        each_peer(lambda d: chunk_copy(kind, m, d, me).start())
        rows[kind, micro_rows(m, me), own_cols] = send[kind, m, slot_rows(me), :]
        relay_copy(kind, m, me, own_cols).start()

    def relay(kind, m):
        def one(block):
            chunk_copy(kind, m, block, block).wait_recv()
            relay_copy(kind, m, block, own_cols).start()

        each_peer(one)

    def arrived(kind, m):
        relay_copy(kind, m, me, other_cols).wait_recv()
        each_peer(lambda block: relay_copy(kind, m, block, other_cols).wait_recv())

    def away_copy(kind, m):
        return pltpu.make_async_remote_copy(
            src_ref=away.at[kind, m],
            dst_ref=recvp.at[kind, m],
            send_sem=s3.at[kind, m],
            recv_sem=r3.at[kind, m],
            device_id={"head": other},
            device_id_type=MESH,
        )

    def back_copy(kind, m, dst, came_from):
        return pltpu.make_async_remote_copy(
            src_ref=keep.at[kind, m, slot_rows(dst), :],
            dst_ref=back.at[kind, m, slot_rows(came_from), :],
            send_sem=s4.at[kind, m, dst],
            recv_sem=r4.at[kind, m, came_from],
            device_id={"expert": dst},
            device_id_type=MESH,
        )

    def send_back(kind, m):
        away_copy(kind, m).wait_recv()
        summed = keep[kind, m].astype(F32) + recvp[kind, m].astype(F32)
        keep[kind, m] = summed.astype(BF16)
        each_peer(lambda d: back_copy(kind, m, d, me).start())
        back[kind, m, slot_rows(me), :] = keep[kind, m, slot_rows(me), :]

    def collect(kind, m):
        each_peer(lambda block: back_copy(kind, m, block, block).wait_recv())
        return dot(tab[m], back[kind, m], TN)

    def section_copy(m):
        return pltpu.make_async_remote_copy(
            src_ref=sec_src.at[m],
            dst_ref=sec_in.at[m],
            send_sem=s5.at[m],
            recv_sem=r5.at[m],
            device_id={"section": 1 - sec},
            device_id_type=MESH,
        )

    def sum_copy(what, m):
        return pltpu.make_async_remote_copy(
            src_ref=xsend.at[what, m],
            dst_ref=xrecv.at[what, m],
            send_sem=s6.at[what, m],
            recv_sem=r6.at[what, m],
            device_id={"head": other},
            device_id_type=MESH,
        )

    def sum_start(what, m, col):
        xsend[what, m] = jnp.broadcast_to(to_row(col), (8, tok))
        sum_copy(what, m).start()

    def sum_done(what, m):
        sum_copy(what, m).wait_recv()
        return to_col(xsend[what, m, 0:1, :] + xrecv[what, m, 0:1, :])

    def square_start(m, tokens):
        values = tokens.astype(F32)
        sum_start(SQUARE, m, jnp.sum(values * values, axis=1, keepdims=True))

    def normalize(m):
        values = rows[FWD, span(m), :].astype(F32)
        inv_scale = lax.rsqrt(jnp.mean(values * values, axis=-1, keepdims=True) + EPSILON)
        normed[span(m), :] = (values * inv_scale * gain).astype(BF16)

    def each_chunk(action):
        def step(c, carry):
            action(pl.ds(pl.multiple_of(c * COLS, COLS), COLS))
            return carry

        lax.fori_loop(0, chunks, step, 0)

    def out_partial(m):
        away[FWD, m] = dot(act[span(m), :], wout_ref[:, other_cols]).astype(BF16)
        away_copy(FWD, m).start()
        keep[FWD, m] = dot(act[span(m), :], wout_ref[:, own_cols]).astype(BF16)

    def grad_partial(m):
        away[BWD, m] = dot(gpre[span(m), :], win_ref[other_cols, :], NT).astype(BF16)
        away_copy(BWD, m).start()
        keep[BWD, m] = dot(gpre[span(m), :], win_ref[own_cols, :], NT).astype(BF16)

    def layer_out(m, tokens):
        return (tokens.astype(F32) + prob[m] * collect(FWD, m)).astype(BF16)

    def sent_grad(m, cot):
        return (prob[m] * cot.astype(F32)).astype(BF16)

    def cross_start(m, tokens):
        scaled = gain_half * collect(BWD, m)
        sum_start(CROSS, m, jnp.sum(scaled * tokens.astype(F32), axis=1, keepdims=True))
        return scaled

    def layer_grad(m, tokens, cot, scaled):
        inv = lax.rsqrt(sum_done(SQUARE, m) / full + EPSILON)
        cross = sum_done(CROSS, m)
        values = tokens.astype(F32)
        return (
            cot.astype(F32) + inv * scaled - values * (inv * inv * inv * cross / full)
        ).astype(BF16)

    def weight_grads():
        def first(c, carry):
            part = pl.ds(pl.multiple_of(c * COLS, COLS), COLS)
            gin_ref[part, :] = dot(normed[:, part], gpre[...], TN).astype(BF16)
            return carry

        lax.fori_loop(0, full // COLS, first, 0)

        def second(part):
            gout_ref[part, :] = dot(act[:, part], rows[BWD], TN).astype(BF16)

        each_chunk(second)


    @pl.when(sec == 0)
    def _():
        for m in range(micro):
            place(FWD, m, local_ref[m])
        pl.semaphore_wait(barrier, experts + 1)
        for m in range(micro):
            dispatch(FWD, m)
        for m in range(micro):
            square_start(m, local_ref[m])

        def forward(m):
            arrived(FWD, m)
            normalize(m)

            def chunk(part):
                pre = dot(normed[span(m), :], win_ref[:, part])
                value, slope = activate(pre)
                act[span(m), part] = value.astype(BF16)
                mid[span(m), part] = slope.astype(mid.dtype)

            each_chunk(chunk)
            out_partial(m)

        def hidden(m):
            sec_src[m] = layer_out(m, local_ref[m])
            section_copy(m).start()

        relay(FWD, 0)
        forward(0)
        relay(FWD, 1)
        send_back(FWD, 0)
        forward(1)
        hidden(0)
        send_back(FWD, 1)
        hidden(1)

        def grad_in(m):
            section_copy(m).wait_recv()
            place(BWD, m, sent_grad(m, sec_in[m]))
            dispatch(BWD, m)

        def backward(m):
            arrived(BWD, m)

            def chunk(part):
                grad_act = dot(rows[BWD, span(m), :], wout_ref[part, :], NT)
                gpre[span(m), part] = (grad_act * mid[span(m), part].astype(F32)).astype(BF16)

            each_chunk(chunk)
            grad_partial(m)

        grad_in(0)
        relay(BWD, 0)
        backward(0)
        grad_in(1)
        send_back(BWD, 0)
        relay(BWD, 1)
        backward(1)
        scaled0 = cross_start(0, local_ref[0])
        send_back(BWD, 1)
        out_ref[0] = layer_grad(0, local_ref[0], sec_in[0], scaled0)
        weight_grads()
        scaled1 = cross_start(1, local_ref[1])
        out_ref[1] = layer_grad(1, local_ref[1], sec_in[1], scaled1)

    @pl.when(sec != 0)
    def _():
        for m in range(micro):
            place(BWD, m, sent_grad(m, local_ref[m]))
        pl.semaphore_wait(barrier, experts + 1)
        for m in range(micro):
            dispatch(BWD, m)
        for m in range(micro):
            relay(BWD, m)
        for m in range(micro):
            arrived(BWD, m)

            def early(part):
                grad_act = dot(rows[BWD, span(m), :], wout_ref[part, :], NT)
                mid[span(m), part] = grad_act.astype(mid.dtype)

            each_chunk(early)

        def hidden_in(m):
            section_copy(m).wait_recv()
            place(FWD, m, sec_in[m])
            dispatch(FWD, m)
            square_start(m, sec_in[m])

        def both(m):
            arrived(FWD, m)
            normalize(m)

            def chunk(part):
                pre = dot(normed[span(m), :], win_ref[:, part])
                value, slope = activate(pre)
                act[span(m), part] = value.astype(BF16)
                gpre[span(m), part] = (mid[span(m), part].astype(F32) * slope).astype(BF16)

            each_chunk(chunk)
            grad_partial(m)

        def finish(m, scaled):
            sec_src[m] = layer_grad(m, sec_in[m], local_ref[m], scaled)
            section_copy(m).start()

        hidden_in(0)
        relay(FWD, 0)
        both(0)
        hidden_in(1)
        send_back(BWD, 0)
        relay(FWD, 1)
        both(1)
        scaled0 = cross_start(0, sec_in[0])
        send_back(BWD, 1)
        finish(0, scaled0)
        out_partial(0)
        scaled1 = cross_start(1, sec_in[1])
        send_back(FWD, 0)
        finish(1, scaled1)
        out_partial(1)
        send_back(FWD, 1)
        weight_grads()
        for m in range(micro):
            out_ref[m] = layer_out(m, sec_in[m])

    for m in range(micro):
        for kind in (FWD, BWD):
            def drain(block):
                chunk_copy(kind, m, block, me).wait_send()
                relay_copy(kind, m, block, own_cols).wait_send()
                back_copy(kind, m, block, me).wait_send()

            each_peer(drain)
            relay_copy(kind, m, me, own_cols).wait_send()
            away_copy(kind, m).wait_send()
        section_copy(m).wait_send()
        sum_copy(SQUARE, m).wait_send()
        sum_copy(CROSS, m).wait_send()


def on_device(boundary, norm_gain, gate_prob, expert_ids, slot_ids, weight_in, weight_out):
    experts = lax.axis_size("expert")
    micro, tok, half = boundary.shape[1:]
    full, hidden_half = weight_in.shape[2:]
    cap = 2 * tok // experts
    pad = -(-cap // 16) * 16
    total = experts * pad
    mid_type = F32 if total <= 512 else BF16
    vmem = pl.BlockSpec(memory_space=pltpu.VMEM)
    per_block = pltpu.SemaphoreType.DMA((2, micro, experts))
    per_pair = pltpu.SemaphoreType.DMA((2, micro))
    per_micro = pltpu.SemaphoreType.DMA((micro,))
    pieces = pltpu.VMEM((2, micro, total, half), BF16)
    tokens = pltpu.VMEM((micro, tok, half), BF16)
    sums = pltpu.VMEM((2, micro, 8, tok), F32)
    out, grad_in, grad_out = pl.pallas_call(
        functools.partial(kernel, experts, cap, pad),
        out_shape=(
            jax.ShapeDtypeStruct((micro, tok, half), BF16),
            jax.ShapeDtypeStruct((full, hidden_half), BF16),
            jax.ShapeDtypeStruct((hidden_half, full), BF16),
        ),
        in_specs=[vmem] * 7,
        out_specs=(vmem, vmem, vmem),
        scratch_shapes=[
            pltpu.VMEM((micro, total, tok), BF16),
            pieces,
            pltpu.VMEM((2, micro * total, full), BF16),
            pltpu.VMEM((micro * total, full), BF16),
            pltpu.VMEM((micro * total, hidden_half), BF16),
            pltpu.VMEM((micro * total, hidden_half), BF16),
            pltpu.VMEM((micro * total, hidden_half), mid_type),
            pieces,
            pieces,
            pieces,
            pieces,
            tokens,
            tokens,
            sums,
            sums,
            per_block, per_block,
            per_block, per_block,
            per_pair, per_pair,
            per_block, per_block,
            per_micro, per_micro,
            per_pair, per_pair,
        ],
        compiler_params=pltpu.CompilerParams(collective_id=0, has_side_effects=True),
    )(
        boundary[0], norm_gain, gate_prob[0], expert_ids[0], slot_ids[0],
        weight_in[0, 0], weight_out[0, 0],
    )
    return (out[None], grad_in[None, None], grad_out[None, None])


def solution(mesh):
    placed = (
        P("section", None, "expert", "head"),
        P("section", None),
        P("section", None, "expert"),
        P("section", None, "expert"),
        P("section", None, "expert"),
        P("section", "expert", None, "head"),
        P("section", "expert", "head", None),
    )
    return jax.shard_map(
        on_device,
        mesh=mesh,
        in_specs=placed,
        out_specs=(
            P("section", None, "expert", "head"),
            P("section", "expert", None, "head"),
            P("section", "expert", "head", None),
        ),
        check_vma=False,
    )
```

profile of v0, /device:TPU:0, one launch (start us, length us, event | category | flops | bytes accessed | tf_op | source)
XLA Modules:
  0.0 114.2 jit_solution(4076625893516411226)
XLA Ops:
  0.6 107.2 %shard_map.94 = (bf16[2,128,384]{2,1,0:T(8,128)(2,1)}, bf16[768,1536]{1,0:T(8,128)(2,1)}, bf16[1536,768]{1,0:T(8,128)(2,1)}) custom-call(bf16[2,128,384]{2,1,0:T(8,128)(2,1)} %bitcast.14, f32[1,768]{1,0:T(1,128)} %gain_ref.1, f32[2,128]{1,0:T(2,128)} %bitcast.15, s32[2,128]{1,0:T(2,128)} %bitcast.16, s32[2,128]{1,0:T(2,128)} %bitcast.17, ...), custom_call_target="tpu_custom_call" | custom-call | tf_op jit(solution)/shard_map/pallas_call | solution.py:411
  107.8 1.6 %copy.13 = bf16[1,2,128,384]{3,2,1,0:T(8,128)(2,1)} copy(bf16[1,2,128,384]{3,2,1,0:T(8,128)(2,1)} %bitcast.13) | data formatting | bytes 393216
  109.4 0.0 copy-start
  109.4 3.4 %copy.14 = bf16[1,1,768,1536]{3,2,1,0:T(8,128)(2,1)} copy(bf16[1,1,768,1536]{3,2,1,0:T(8,128)(2,1)} %bitcast.10) | data formatting | bytes 4718592
  112.8 0.0 copy-done
  112.8 1.4 %copy.15 = bf16[1,1,1536,768]{3,2,1,0:T(8,128)(2,1)} copy(bf16[1,1,1536,768]{3,2,1,0:T(8,128)(2,1)S(1)} %bitcast.9) | data formatting | bytes 4718592
Async XLA Ops:
  109.4 3.4 %copy-start = (bf16[1536,768]{1,0:T(8,128)(2,1)S(1)}, bf16[1536,768]{1,0:T(8,128)(2,1)}, u32[]{:S(2)}) copy-start(bf16[1536,768]{1,0:T(8,128)(2,1)} %get-tuple-element.8) | copy-start | bytes 7077892
where the time goes:
time: 114 us
  Pallas kernels  107 us (94%)
  local copies, waits for them, and re-layouts  6.4 us (6%)
    pallas_call x1, Pallas kernels, on_device(): pl.pallas_call(functools.partial(kernel, experts, cap, pad), out_shape=(j...  107 us
    unnamed x5, local copies, waits for them, and re-layouts  6.4 us

commit v1 on v0

--- a/solution.py
+++ b/solution.py
@@ -16,6 +16,9 @@
 FWD, BWD = 0, 1
 SQUARE, CROSS = 0, 1
 COLS = 256
+SPLIT = 2
+VMEM_LIMIT = 56 * 2**20
+COPY_LIMIT = 2**20
 
 
 def activate(pre_act):
@@ -37,11 +40,16 @@
 
 def kernel(
     experts, cap, pad,
-    local_ref, gain_ref, prob_ref, ids_ref, slots_ref, win_ref, wout_ref,
+    local_ref, gain_ref, prob_ref, ids_ref, slots_ref, win_hbm, wout_hbm,
     out_ref, gin_ref, gout_ref,
     tab, send, rows, normed, act, gpre, mid, keep, away, recvp, back, sec_src, sec_in, xsend, xrecv,
+    win_ref, wout_ref, load_sem,
     s1, r1, s2, r2, s3, r3, s4, r4, s5, r5, s6, r6,
 ):
+    win_load = pltpu.make_async_copy(win_hbm, win_ref, load_sem.at[0])
+    wout_load = pltpu.make_async_copy(wout_hbm, wout_ref, load_sem.at[1])
+    win_load.start()
+    wout_load.start()
     sec, me, head = lax.axis_index("section"), lax.axis_index("expert"), lax.axis_index("head")
     other = 1 - head
     micro, tok, half = local_ref.shape
@@ -61,9 +69,13 @@
 
         lax.fori_loop(1, experts, step, 0)
 
-    each_peer(
-        lambda d: pl.semaphore_signal(barrier, inc=1, device_id={"expert": d}, device_id_type=MESH)
-    )
+    def greet(d):
+        for h in range(2):
+            pl.semaphore_signal(
+                barrier, inc=1, device_id={"expert": d, "head": h}, device_id_type=MESH
+            )
+
+    each_peer(greet)
     pl.semaphore_signal(barrier, inc=1, device_id={"head": other}, device_id_type=MESH)
     pl.semaphore_signal(barrier, inc=1, device_id={"section": 1 - sec}, device_id_type=MESH)
 
@@ -105,13 +117,13 @@
             device_id_type=MESH,
         )
 
-    def relay_copy(kind, m, block, cols):
+    def cross_copy(kind, m, dst, came_from, cols):
         return pltpu.make_async_remote_copy(
-            src_ref=rows.at[kind, micro_rows(m, block), own_cols],
-            dst_ref=rows.at[kind, micro_rows(m, block), cols],
-            send_sem=s2.at[kind, m, block],
-            recv_sem=r2.at[kind, m, block],
-            device_id={"head": other},
+            src_ref=send.at[kind, m, slot_rows(dst), :],
+            dst_ref=rows.at[kind, micro_rows(m, came_from), cols],
+            send_sem=s2.at[kind, m, dst],
+            recv_sem=r2.at[kind, m, came_from],
+            device_id={"expert": dst, "head": other},
             device_id_type=MESH,
         )
 
@@ -119,27 +131,34 @@
         send[kind, m] = dot(tab[m], tokens).astype(BF16)
 
     def dispatch(kind, m):
-        each_peer(lambda d: chunk_copy(kind, m, d, me).start())
+        def both_heads(d):
+            cross_copy(kind, m, d, me, own_cols).start()
+            chunk_copy(kind, m, d, me).start()
+
+        each_peer(both_heads)
+        cross_copy(kind, m, me, me, own_cols).start()
         rows[kind, micro_rows(m, me), own_cols] = send[kind, m, slot_rows(me), :]
-        relay_copy(kind, m, me, own_cols).start()
-
-    def relay(kind, m):
-        def one(block):
+
+    def arrived(kind, m):
+        def both_heads(block):
             chunk_copy(kind, m, block, block).wait_recv()
-            relay_copy(kind, m, block, own_cols).start()
-
-        each_peer(one)
-
-    def arrived(kind, m):
-        relay_copy(kind, m, me, other_cols).wait_recv()
-        each_peer(lambda block: relay_copy(kind, m, block, other_cols).wait_recv())
-
-    def away_copy(kind, m):
+            cross_copy(kind, m, block, block, other_cols).wait_recv()
+
+        cross_copy(kind, m, me, me, other_cols).wait_recv()
+        each_peer(both_heads)
+
+    def piece(c):
+        return slice(c * (total // SPLIT), (c + 1) * (total // SPLIT))
+
+    def piece_of(m, c):
+        return slice(m * total + c * (total // SPLIT), m * total + (c + 1) * (total // SPLIT))
+
+    def away_copy(kind, m, c):
         return pltpu.make_async_remote_copy(
-            src_ref=away.at[kind, m],
-            dst_ref=recvp.at[kind, m],
-            send_sem=s3.at[kind, m],
-            recv_sem=r3.at[kind, m],
+            src_ref=away.at[kind, m, piece(c), :],
+            dst_ref=recvp.at[kind, m, piece(c), :],
+            send_sem=s3.at[kind, m, c],
+            recv_sem=r3.at[kind, m, c],
             device_id={"head": other},
             device_id_type=MESH,
         )
@@ -155,10 +174,19 @@
         )
 
     def send_back(kind, m):
-        away_copy(kind, m).wait_recv()
-        summed = keep[kind, m].astype(F32) + recvp[kind, m].astype(F32)
-        keep[kind, m] = summed.astype(BF16)
-        each_peer(lambda d: back_copy(kind, m, d, me).start())
+        for c in range(SPLIT):
+            away_copy(kind, m, c).wait_recv()
+            summed = keep[kind, m, piece(c), :].astype(F32) + recvp[kind, m, piece(c), :].astype(F32)
+            keep[kind, m, piece(c), :] = summed.astype(BF16)
+
+            def one(dst, carry):
+                @pl.when(dst != me)
+                def _():
+                    back_copy(kind, m, dst, me).start()
+
+                return carry
+
+            lax.fori_loop(c * experts // SPLIT, (c + 1) * experts // SPLIT, one, 0)
         back[kind, m, slot_rows(me), :] = keep[kind, m, slot_rows(me), :]
 
     def collect(kind, m):
@@ -210,13 +238,19 @@
         lax.fori_loop(0, chunks, step, 0)
 
     def out_partial(m):
-        away[FWD, m] = dot(act[span(m), :], wout_ref[:, other_cols]).astype(BF16)
-        away_copy(FWD, m).start()
+        for c in range(SPLIT):
+            away[FWD, m, piece(c), :] = dot(act[piece_of(m, c), :], wout_ref[:, other_cols]).astype(
+                BF16
+            )
+            away_copy(FWD, m, c).start()
         keep[FWD, m] = dot(act[span(m), :], wout_ref[:, own_cols]).astype(BF16)
 
     def grad_partial(m):
-        away[BWD, m] = dot(gpre[span(m), :], win_ref[other_cols, :], NT).astype(BF16)
-        away_copy(BWD, m).start()
+        for c in range(SPLIT):
+            away[BWD, m, piece(c), :] = dot(gpre[piece_of(m, c), :], win_ref[other_cols, :], NT).astype(
+                BF16
+            )
+            away_copy(BWD, m, c).start()
         keep[BWD, m] = dot(gpre[span(m), :], win_ref[own_cols, :], NT).astype(BF16)
 
     def layer_out(m, tokens):
@@ -256,11 +290,13 @@
     def _():
         for m in range(micro):
             place(FWD, m, local_ref[m])
-        pl.semaphore_wait(barrier, experts + 1)
+        pl.semaphore_wait(barrier, 2 * experts)
         for m in range(micro):
             dispatch(FWD, m)
         for m in range(micro):
             square_start(m, local_ref[m])
+        win_load.wait()
+        wout_load.wait()
 
         def forward(m):
             arrived(FWD, m)
@@ -279,9 +315,7 @@
             sec_src[m] = layer_out(m, local_ref[m])
             section_copy(m).start()
 
-        relay(FWD, 0)
         forward(0)
-        relay(FWD, 1)
         send_back(FWD, 0)
         forward(1)
         hidden(0)
@@ -304,11 +338,9 @@
             grad_partial(m)
 
         grad_in(0)
-        relay(BWD, 0)
         backward(0)
         grad_in(1)
         send_back(BWD, 0)
-        relay(BWD, 1)
         backward(1)
         scaled0 = cross_start(0, local_ref[0])
         send_back(BWD, 1)
@@ -321,11 +353,11 @@
     def _():
         for m in range(micro):
             place(BWD, m, sent_grad(m, local_ref[m]))
-        pl.semaphore_wait(barrier, experts + 1)
+        pl.semaphore_wait(barrier, 2 * experts)
         for m in range(micro):
             dispatch(BWD, m)
-        for m in range(micro):
-            relay(BWD, m)
+        win_load.wait()
+        wout_load.wait()
         for m in range(micro):
             arrived(BWD, m)
 
@@ -359,11 +391,9 @@
             section_copy(m).start()
 
         hidden_in(0)
-        relay(FWD, 0)
         both(0)
         hidden_in(1)
         send_back(BWD, 0)
-        relay(FWD, 1)
         both(1)
         scaled0 = cross_start(0, sec_in[0])
         send_back(BWD, 1)
@@ -382,15 +412,25 @@
         for kind in (FWD, BWD):
             def drain(block):
                 chunk_copy(kind, m, block, me).wait_send()
-                relay_copy(kind, m, block, own_cols).wait_send()
+                cross_copy(kind, m, block, me, own_cols).wait_send()
                 back_copy(kind, m, block, me).wait_send()
 
             each_peer(drain)
-            relay_copy(kind, m, me, own_cols).wait_send()
-            away_copy(kind, m).wait_send()
+            cross_copy(kind, m, me, me, own_cols).wait_send()
+            for c in range(SPLIT):
+                away_copy(kind, m, c).wait_send()
         section_copy(m).wait_send()
         sum_copy(SQUARE, m).wait_send()
         sum_copy(CROSS, m).wait_send()
+
+
+def copy_out(out_in, gin_in, gout_in, out_ref, gin_ref, gout_ref, sem):
+    pairs = ((gin_in, gin_ref), (gout_in, gout_ref), (out_in, out_ref))
+    copies = [pltpu.make_async_copy(a, b, sem.at[i]) for i, (a, b) in enumerate(pairs)]
+    for copy in copies:
+        copy.start()
+    for copy in copies:
+        copy.wait()
 
 
 def on_device(boundary, norm_gain, gate_prob, expert_ids, slot_ids, weight_in, weight_out):
@@ -402,8 +442,10 @@
     total = experts * pad
     mid_type = F32 if total <= 512 else BF16
     vmem = pl.BlockSpec(memory_space=pltpu.VMEM)
+    anywhere = pl.BlockSpec(memory_space=pl.ANY)
     per_block = pltpu.SemaphoreType.DMA((2, micro, experts))
     per_pair = pltpu.SemaphoreType.DMA((2, micro))
+    per_piece = pltpu.SemaphoreType.DMA((2, micro, SPLIT))
     per_micro = pltpu.SemaphoreType.DMA((micro,))
     pieces = pltpu.VMEM((2, micro, total, half), BF16)
     tokens = pltpu.VMEM((micro, tok, half), BF16)
@@ -411,11 +453,11 @@
     out, grad_in, grad_out = pl.pallas_call(
         functools.partial(kernel, experts, cap, pad),
         out_shape=(
-            jax.ShapeDtypeStruct((micro, tok, half), BF16),
-            jax.ShapeDtypeStruct((full, hidden_half), BF16),
-            jax.ShapeDtypeStruct((hidden_half, full), BF16),
+            pltpu.VMEM((micro, tok, half), BF16),
+            pltpu.VMEM((full, hidden_half), BF16),
+            pltpu.VMEM((hidden_half, full), BF16),
         ),
-        in_specs=[vmem] * 7,
+        in_specs=[vmem] * 5 + [anywhere] * 2,
         out_specs=(vmem, vmem, vmem),
         scratch_shapes=[
             pltpu.VMEM((micro, total, tok), BF16),
@@ -433,18 +475,32 @@
             tokens,
             sums,
             sums,
+            pltpu.VMEM((full, hidden_half), BF16),
+            pltpu.VMEM((hidden_half, full), BF16),
+            pltpu.SemaphoreType.DMA((2,)),
             per_block, per_block,
             per_block, per_block,
-            per_pair, per_pair,
+            per_piece, per_piece,
             per_block, per_block,
             per_micro, per_micro,
             per_pair, per_pair,
         ],
-        compiler_params=pltpu.CompilerParams(collective_id=0, has_side_effects=True),
+        compiler_params=pltpu.CompilerParams(
+            collective_id=0, has_side_effects=True, vmem_limit_bytes=VMEM_LIMIT
+        ),
     )(
         boundary[0], norm_gain, gate_prob[0], expert_ids[0], slot_ids[0],
         weight_in[0, 0], weight_out[0, 0],
     )
+    results = (out, grad_in, grad_out)
+    out, grad_in, grad_out = pl.pallas_call(
+        copy_out,
+        out_shape=[jax.ShapeDtypeStruct(x.shape, x.dtype) for x in results],
+        in_specs=[vmem] * 3,
+        out_specs=[anywhere] * 3,
+        scratch_shapes=[pltpu.SemaphoreType.DMA((3,))],
+        compiler_params=pltpu.CompilerParams(vmem_limit_bytes=COPY_LIMIT),
+    )(*results)
     return (out[None], grad_in[None, None], grad_out[None, None])
 
 

time: 114 us -> 102 us (0.89)
  local copies, waits for them, and re-layouts: 6.4 us -> 0 us
  Pallas kernels: 107 us -> 101 us
    unnamed x5 -> x0, local copies, waits for them, and re-layouts: 6.4 us -> none
    pallas_call x1 -> x2, Pallas kernels: 107 us -> 101 us  [the longest x1 99.2 us: on_device(): pl.pallas_call(functools.partial(kernel, experts, cap, pad), out_shape=(p...]
where the time goes in v1:
time: 102 us
  Pallas kernels  101 us (99%)
    pallas_call x1, Pallas kernels, on_device(): pl.pallas_call(functools.partial(kernel, experts, cap, pad), out_shape=(p...  99.2 us
    pallas_call x1, Pallas kernels, on_device(): pl.pallas_call(copy_out, out_shape=[jax.ShapeDtypeStruct(x.shape, x.dtype...  2.26 us

profile of v1, /device:TPU:0, one launch (start us, length us, event | category | flops | bytes accessed | tf_op | source)
XLA Modules:
  0.0 102.2 jit_solution(11219978632681069279)
XLA Ops:
  0.6 99.2 %shard_map.94 = (bf16[2,128,384]{2,1,0:T(8,128)(2,1)S(1)}, bf16[768,1536]{1,0:T(8,128)(2,1)S(1)}, bf16[1536,768]{1,0:T(8,128)(2,1)S(1)}) custom-call(bf16[2,128,384]{2,1,0:T(8,128)(2,1)} %bitcast.11, f32[1,768]{1,0:T(1,128)} %gain_ref.1, f32[2,128]{1,0:T(2,128)} %bitcast.12, s32[2,128]{1,0:T(2,128)} %bitcast.13, s32[2,128]{1,0:T(2,128)} %bitcast.14, ...), custom_call_target="tpu_custom_call" | custom-call | tf_op jit(solution)/shard_map/pallas_call | solution.py:453
  99.8 2.3 %shard_map.95 = (bf16[2,128,384]{2,1,0:T(8,128)(2,1)}, bf16[768,1536]{1,0:T(8,128)(2,1)}, bf16[1536,768]{1,0:T(8,128)(2,1)}) custom-call(bf16[2,128,384]{2,1,0:T(8,128)(2,1)S(1)} %get-tuple-element.9.out_in, bf16[768,1536]{1,0:T(8,128)(2,1)S(1)} %get-tuple-element.10.gin_in, bf16[1536,768]{1,0:T(8,128)(2,1)S(1)} %get-tuple-element.11.gout_in), custom_call_target="tpu_custom_call" | custom-call | tf_op jit(solution)/shard_map/pallas_call | solution.py:496

commit v2 on v1

--- a/solution.py
+++ b/solution.py
@@ -43,7 +43,7 @@
     local_ref, gain_ref, prob_ref, ids_ref, slots_ref, win_hbm, wout_hbm,
     out_ref, gin_ref, gout_ref,
     tab, send, rows, normed, act, gpre, mid, keep, away, recvp, back, sec_src, sec_in, xsend, xrecv,
-    win_ref, wout_ref, load_sem,
+    win_ref, wout_ref, load_sem, turn,
     s1, r1, s2, r2, s3, r3, s4, r4, s5, r5, s6, r6,
 ):
     win_load = pltpu.make_async_copy(win_hbm, win_ref, load_sem.at[0])
@@ -300,6 +300,9 @@
 
         def forward(m):
             arrived(FWD, m)
+            pl.semaphore_signal(
+                turn.at[m], inc=1, device_id={"section": 1 - sec}, device_id_type=MESH
+            )
             normalize(m)
 
             def chunk(part):
@@ -354,11 +357,13 @@
         for m in range(micro):
             place(BWD, m, sent_grad(m, local_ref[m]))
         pl.semaphore_wait(barrier, 2 * experts)
-        for m in range(micro):
-            dispatch(BWD, m)
         win_load.wait()
         wout_load.wait()
         for m in range(micro):
+            pl.semaphore_wait(turn.at[m], 1)
+            dispatch(BWD, m)
+
+        def early_grad(m):
             arrived(BWD, m)
 
             def early(part):
@@ -366,6 +371,9 @@
                 mid[span(m), part] = grad_act.astype(mid.dtype)
 
             each_chunk(early)
+
+        for m in range(micro):
+            early_grad(m)
 
         def hidden_in(m):
             section_copy(m).wait_recv()
@@ -478,6 +486,7 @@
             pltpu.VMEM((full, hidden_half), BF16),
             pltpu.VMEM((hidden_half, full), BF16),
             pltpu.SemaphoreType.DMA((2,)),
+            pltpu.SemaphoreType.REGULAR((micro,)),
             per_block, per_block,
             per_block, per_block,
             per_piece, per_piece,

time: 102 us -> 99 us (0.971)
  Pallas kernels: 101 us -> 98 us
    pallas_call x1, Pallas kernels: 99.2 us -> 95.8 us  [on_device(): pl.pallas_call(functools.partial(kernel, experts, cap, pad), out_shape=(p...]
where the time goes in v2:
time: 99 us; the launch traced here: 98.8 us
  Pallas kernels  98 us (99%)
    pallas_call x1, Pallas kernels, on_device(): pl.pallas_call(functools.partial(kernel, experts, cap, pad), out_shape=(p...  95.8 us
    pallas_call x1, Pallas kernels, on_device(): pl.pallas_call(copy_out, out_shape=[jax.ShapeDtypeStruct(x.shape, x.dtype...  2.26 us

profile of v2, /device:TPU:0, one launch (start us, length us, event | category | flops | bytes accessed | tf_op | source)
XLA Modules:
  0.0 98.8 jit_solution(5131857220300793160)
XLA Ops:
  0.6 95.8 %shard_map.94 = (bf16[2,128,384]{2,1,0:T(8,128)(2,1)S(1)}, bf16[768,1536]{1,0:T(8,128)(2,1)S(1)}, bf16[1536,768]{1,0:T(8,128)(2,1)S(1)}) custom-call(bf16[2,128,384]{2,1,0:T(8,128)(2,1)} %bitcast.11, f32[1,768]{1,0:T(1,128)} %gain_ref.1, f32[2,128]{1,0:T(2,128)} %bitcast.12, s32[2,128]{1,0:T(2,128)} %bitcast.13, s32[2,128]{1,0:T(2,128)} %bitcast.14, ...), custom_call_target="tpu_custom_call" | custom-call | tf_op jit(solution)/shard_map/pallas_call | solution.py:461
  96.4 2.3 %shard_map.95 = (bf16[2,128,384]{2,1,0:T(8,128)(2,1)}, bf16[768,1536]{1,0:T(8,128)(2,1)}, bf16[1536,768]{1,0:T(8,128)(2,1)}) custom-call(bf16[2,128,384]{2,1,0:T(8,128)(2,1)S(1)} %get-tuple-element.9.out_in, bf16[768,1536]{1,0:T(8,128)(2,1)S(1)} %get-tuple-element.10.gin_in, bf16[1536,768]{1,0:T(8,128)(2,1)S(1)} %get-tuple-element.11.gout_in), custom_call_target="tpu_custom_call" | custom-call | tf_op jit(solution)/shard_map/pallas_call | solution.py:505
